TPU v7x, 32 devices: a whole 2x2x4 slice. The times are simulated.
32 devices in a mesh: dp: 8 (over z, y), hg: 2 (over x), hid: 2 (over core).
Axes of the slice: x: 2, y: 2, z: 4, core: 2. Of those that a mesh axis runs over, the one named last changes fastest.
Arguments:
- tokens: bfloat16 [18816, 768], P(('dp', 'hid')), may hold values from -6 to 6
- big_images: int32 [16], P(('dp', 'hid')), may hold values from 0 to 1, as said below
- norm_gain: bfloat16 [768], replicated, may hold values from 0.5 to 1.5
- w_qkv: bfloat16 [768, 2304], P(None, 'hg'), may hold values from -0.21875 to 0.21875
- qk_gains: bfloat16 [2, 64], replicated, may hold values from 0.099609375 to 1.8984375
- w_out_t: bfloat16 [768, 768], P(None, 'hg'), may hold values from -0.625 to 0.625
- w_in: bfloat16 [768, 3072], P(None, ('hg', 'hid')), may hold values from -0.21875 to 0.21875
- w_back: bfloat16 [768, 3072], P(None, ('hg', 'hid')), may hold values from -0.109375 to 0.109375
- cotangent: bfloat16 [18816, 768], P(('dp', 'hid'), 'hg'), may hold values from -6 to 6
Outputs:
- output: bfloat16 [18816, 768], P(('dp', 'hid'), 'hg')
- token_grad: bfloat16 [18816, 768], P(('dp', 'hid'))
- norm_gain_grad: float32 [768], P(('dp', 'hid'))
- w_qkv_grad: float32 [768, 2304], P(('dp', 'hid'), 'hg')
- qk_gains_grad: float32 [2, 64], replicated
- w_out_t_grad: float32 [768, 768], P(('dp', 'hid'), 'hg')
- w_in_grad: float32 [768, 3072], P('dp', ('hg', 'hid'))
- w_back_grad: float32 [768, 3072], P('dp', ('hg', 'hid'))
Inputs may be any that keep to these rules, and one draw needn't show every extreme that they name: `big_images`: 1 where the 1176 tokens of a group form one image, 0 where they form 6 images of 196 tokens each in order; every draw has groups of both kinds.
All inputs are finite; a program needn't handle non-finite values.
Results may differ from a plain program's by a relative error of at most 0.012.
Values may be sent and summed in bfloat16 or wider, within the bound.
No kernel may reach another device: no remote copies, remote signals or barrier semaphores. Data moves between devices by JAX's collectives and lax.ppermute only.
A program may use at most 256 MiB of HBM per device.

v0:
```python
import jax
import jax.numpy as jnp
from jax import lax
from jax.sharding import PartitionSpec as P

PATCHES = 196
EPSILON = 1e-06


def normalize(values):
    centred = values - jnp.mean(values, axis=-1, keepdims=True)
    inverse = lax.rsqrt(jnp.mean(centred * centred, axis=-1, keepdims=True) + EPSILON)
    return (centred * inverse, inverse)


def normalize_back(upstream, normed, inverse):
    inner = jnp.mean(upstream * normed, axis=-1, keepdims=True)
    return inverse * (upstream - jnp.mean(upstream, axis=-1, keepdims=True) - normed * inner)


def times_t(left, right):
    return lax.dot_general(
        left, right, (((1,), (1,)), ((), ())), preferred_element_type=jnp.float32
    )


def rows_t(left, right):
    return lax.dot_general(
        left, right, (((0,), (0,)), ((), ())), preferred_element_type=jnp.float32
    )


def masked_scores(queries, keys_in, allowed):
    scores = jnp.einsum("gqe,gke->gqk", queries, keys_in, preferred_element_type=jnp.float32)
    return jnp.where(allowed, scores, -1e30)


def head_forward(queries, keys_in, values_in, allowed):
    scores = masked_scores(queries, keys_in, allowed)
    highest = jnp.max(scores, axis=-1, keepdims=True)
    expo_scores = jnp.exp(scores - highest)
    totals = jnp.sum(expo_scores, axis=-1, keepdims=True)
    weights = (expo_scores / totals).astype(jnp.bfloat16)
    attended = jnp.einsum("gqk,gke->gqe", weights, values_in, preferred_element_type=jnp.float32)
    return (attended, (highest + jnp.log(totals))[..., 0])


def head_back(queries, keys_in, values_in, log_total, grad_out, allowed):
    scores = masked_scores(queries, keys_in, allowed)
    probs = jnp.exp(scores - log_total[..., None])
    grad_probs = jnp.einsum("gqe,gke->gqk", grad_out, values_in, preferred_element_type=jnp.float32)
    inner = jnp.sum(grad_probs * probs, axis=-1, keepdims=True)
    grad_scores = (probs * (grad_probs - inner)).astype(jnp.bfloat16)
    grad_values = jnp.einsum(
        "gqk,gqe->gke", probs.astype(jnp.bfloat16), grad_out, preferred_element_type=jnp.float32
    )
    grad_queries = jnp.einsum(
        "gqk,gke->gqe", grad_scores, keys_in, preferred_element_type=jnp.float32
    )
    grad_keys = jnp.einsum("gqk,gqe->gke", grad_scores, queries, preferred_element_type=jnp.float32)
    return (grad_queries, grad_keys, grad_values)


def attention_pass(step_fn, arrays, big_flag):
    heads_here = arrays[0].shape[0]
    tok_rows = arrays[0].shape[1]
    image_of = jnp.arange(tok_rows) // PATCHES
    allowed = (image_of[:, None] == image_of[None, :]) | (big_flag > 0)
    run_allowed = allowed[None]
    shaped = tuple(
        (member.reshape((heads_here, 1, tok_rows // 1) + member.shape[2:]) for member in arrays)
    )
    results = lax.map(lambda blocks: step_fn(*blocks, run_allowed), shaped)
    return tuple((member.reshape((heads_here, tok_rows) + member.shape[3:]) for member in results))


def shards(tokens, big_images, norm_gain, w_qkv, qk_gains, w_out_t, w_in, w_back, cotangent):
    tok_rows = tokens.shape[0]
    width = tokens.shape[1]
    head_size = qk_gains.shape[1]
    heads_here = w_qkv.shape[1] // (3 * head_size)
    half_width = heads_here * head_size
    big_flag = big_images[0]
    head_scale = head_size ** (-0.5)
    inputs = tokens.astype(jnp.float32)
    normed, inverse = normalize(inputs)
    gain_vec = norm_gain.astype(jnp.float32)
    normed_low = (normed * gain_vec).astype(jnp.bfloat16)
    joined = jnp.dot(normed_low, w_qkv, preferred_element_type=jnp.float32).reshape(
        tok_rows, heads_here, 3, head_size
    )
    q_hat, q_inverse = normalize(joined[:, :, 0])
    k_hat, k_inverse = normalize(joined[:, :, 1])
    q_gain = qk_gains[0].astype(jnp.float32)
    k_gain = qk_gains[1].astype(jnp.float32)
    queries = (q_hat * q_gain * head_scale).astype(jnp.bfloat16).transpose(1, 0, 2)
    keys_in = (k_hat * k_gain).astype(jnp.bfloat16).transpose(1, 0, 2)
    values_in = joined[:, :, 2].astype(jnp.bfloat16).transpose(1, 0, 2)
    attended, log_total = attention_pass(head_forward, (queries, keys_in, values_in), big_flag)
    attended_low = attended.astype(jnp.bfloat16).transpose(1, 0, 2).reshape(tok_rows, half_width)
    attn_part = times_t(attended_low, w_out_t)
    normed_all = lax.all_gather(normed_low, "hid", axis=0, tiled=True)
    hidden_pre = jnp.dot(normed_all, w_in, preferred_element_type=jnp.float32)
    hidden_act = jax.nn.gelu(hidden_pre).astype(jnp.bfloat16)
    mlp_part = lax.psum_scatter(
        times_t(hidden_act, w_back).astype(jnp.bfloat16), "hid", scatter_dimension=0, tiled=True
    ).astype(jnp.float32)
    mixed = lax.psum_scatter(attn_part + mlp_part, "hg", scatter_dimension=1, tiled=True)
    out_cols = width // lax.axis_size("hg")
    input_cols = lax.dynamic_slice_in_dim(inputs, lax.axis_index("hg") * out_cols, out_cols, 1)
    output = (input_cols + mixed).astype(jnp.bfloat16)
    grad_out = lax.all_gather(cotangent, "hg", axis=1, tiled=True)
    grad_w_out = rows_t(grad_out, attended_low)
    grad_attended = jnp.dot(grad_out, w_out_t, preferred_element_type=jnp.float32)
    grad_att_low = (
        grad_attended.astype(jnp.bfloat16)
        .reshape(tok_rows, heads_here, head_size)
        .transpose(1, 0, 2)
    )
    grad_queries, grad_keys, grad_values = attention_pass(
        head_back, (queries, keys_in, values_in, log_total, grad_att_low), big_flag
    )
    grad_query = grad_queries.transpose(1, 0, 2) * head_scale
    grad_key = grad_keys.transpose(1, 0, 2)
    qk_partial = jnp.stack(
        [jnp.sum(grad_query * q_hat, axis=(0, 1)), jnp.sum(grad_key * k_hat, axis=(0, 1))]
    )
    grad_q_raw = normalize_back(grad_query * q_gain, q_hat, q_inverse)
    grad_k_raw = normalize_back(grad_key * k_gain, k_hat, k_inverse)
    grad_joined = jnp.stack([grad_q_raw, grad_k_raw, grad_values.transpose(1, 0, 2)], axis=2)
    grad_joined = grad_joined.reshape(tok_rows, 3 * half_width).astype(jnp.bfloat16)
    grad_w_qkv = rows_t(normed_low, grad_joined)
    grad_normed_att = times_t(grad_joined, w_qkv)
    grad_out_all = lax.all_gather(grad_out, "hid", axis=0, tiled=True)
    grad_act = jnp.dot(grad_out_all, w_back, preferred_element_type=jnp.float32)
    grad_up = jax.vjp(jax.nn.gelu, hidden_pre)[1](grad_act)[0].astype(jnp.bfloat16)
    grad_w_back = rows_t(grad_out_all, hidden_act)
    grad_w_in = rows_t(normed_all, grad_up)
    grad_normed_mlp = lax.psum_scatter(
        times_t(grad_up, w_in).astype(jnp.bfloat16), "hid", scatter_dimension=0, tiled=True
    ).astype(jnp.float32)
    grad_normed = lax.psum(grad_normed_att + grad_normed_mlp, "hg")
    token_grad = (
        normalize_back(grad_normed * gain_vec, normed, inverse) + grad_out.astype(jnp.float32)
    ).astype(jnp.bfloat16)
    gain_partial = jnp.sum(grad_normed * normed, axis=0)
    w_qkv_grad, w_out_t_grad, norm_gain_grad = (
        lax.psum_scatter(grad_w_qkv, ("dp", "hid"), scatter_dimension=0, tiled=True),
        lax.psum_scatter(grad_w_out, ("dp", "hid"), scatter_dimension=0, tiled=True),
        lax.psum_scatter(gain_partial, ("dp", "hid"), scatter_dimension=0, tiled=True),
    )
    w_in_grad, w_back_grad = (
        lax.psum_scatter(
            grad_w_in.astype(jnp.bfloat16), "dp", scatter_dimension=0, tiled=True
        ).astype(jnp.float32),
        lax.psum_scatter(
            grad_w_back.astype(jnp.bfloat16), "dp", scatter_dimension=0, tiled=True
        ).astype(jnp.float32),
    )
    qk_gains_grad = lax.psum(qk_partial, ("dp", "hg", "hid"))
    return (
        output,
        token_grad,
        norm_gain_grad,
        w_qkv_grad,
        qk_gains_grad,
        w_out_t_grad,
        w_in_grad,
        w_back_grad,
    )


def solution(mesh):
    return jax.shard_map(
        shards,
        mesh=mesh,
        in_specs=(
            P(("dp", "hid"), None),
            P(("dp", "hid")),
            P(),
            P(None, "hg"),
            P(),
            P(None, "hg"),
            P(None, ("hg", "hid")),
            P(None, ("hg", "hid")),
            P(("dp", "hid"), "hg"),
        ),
        out_specs=(
            P(("dp", "hid"), "hg"),
            P(("dp", "hid"), None),
            P(("dp", "hid")),
            P(("dp", "hid"), "hg"),
            P(),
            P(("dp", "hid"), "hg"),
            P("dp", ("hg", "hid")),
            P("dp", ("hg", "hid")),
        ),
        check_vma=False,
    )
```

profile of v0, /device:TPU:0, one launch (start us, length us, event | category | flops | bytes accessed | tf_op | source)
XLA Modules:
  0.0 659.5 jit_solution(1568707283787377378)
XLA Ops:
  8.0 34.2 %all-gather.6.cloned.1.call-done = bf16[1176,768]{1,0:T(8,128)(2,1)} async-done(((bf16[1176,384]{1,0:T(8,128)(2,1)}), bf16[1176,768]{1,0:T(8,128)(2,1)}) %all-gather.6.cloned.1.call-update) | async-done | bytes 1806352 | tf_op jit(solution)/shard_map/all_gather | solution.py:112
  48.1 4.0 fusion.76
  52.3 2.5 copy-done.1
  55.1 2.7 multiply_reduce_fusion.6
  57.8 3.8 fusion.66
  61.7 3.2 copy.43
  71.0 8.3 %fusion.77 = f32[2352,768]{1,0:T(8,128)} fusion(bf16[2352,768]{1,0:T(8,128)(2,1)} %all-gather.8.cloned.1.call-done, bf16[768,768]{1,0:T(8,128)(2,1)} %param.20), kind=kOutput, calls=%fused_computation.143 | convolution fusion | flops 2774532096 | bytes 12017664 | tf_op jit(solution)/shard_map/dot_general | solution.py:135
  79.3 11.3 %fusion.54 = (bf16[2352,768]{1,0:T(8,128)(2,1)S(1)}, f32[2352,768]{1,0:T(8,128)}) fusion(f32[2352,768]{1,0:T(8,128)} %fusion.77, bf16[2352,768]{1,0:T(8,128)(2,1)} %all-gather.4.cloned.1.call-done, bf16[768,768]{1,0:T(8,128)(2,1)} %param.19), kind=kOutput, calls=%fused_computation.61 | convolution fusion | flops 2810658816 | bytes 22855680 | tf_op jit(solution)/shard_map/dot_general | solution.py:103
  92.5 4.6 convolution_convert_fusion
  98.3 33.6 %while.30 = (s32[]{:T(128)}, bf16[6,1,1176,64]{2,3,1,0:T(8,128)(2,1)S(1)}, f32[6,1,1176]{2,1,0:T(1,128)S(1)}, bf16[6,1,1176,64]{3,2,1,0:T(8,128)(2,1)}, bf16[6,1...) while((s32[]{:T(128)}, ...), condition=%wide.region_9.10_spmd.clone.clone, body=%wide.region_6.9_spmd.clone.sunk.clone | while | flops 366487456 | bytes 18392728 | solution.py:73
  98.5 2.5 fusion.136
  104.0 2.5 fusion.136
  120.8 2.5 fusion.136
  132.5 3.5 convolution_convert_fusion.2
  138.2 9.6 %convolution_convert_fusion.1 = bf16[2352,768]{1,0:T(8,128)(2,1)} fusion(bf16[768,768]{1,0:T(8,128)(2,1)} %param.20, f32[2352,768]{1,0:T(8,128)} %get-tuple-element.296), kind=kOutput, calls=%fused_computation.64 | convolution fusion | flops 2792595456 | bytes 12017664 | tf_op jit(solution)/shard_map/dot_general | solution.py:22
  149.1 79.0 %while.31 = (s32[]{:T(128)}, f32[6,1,1176,64]{2,3,1,0:T(8,128)}, f32[6,1,1176,64]{2,3,1,0:T(8,128)}, bf16[6,1,1176,64]{2,3,1,0:T(8,128)(2,1)S(1)}, bf16[6,1,1176...) while((s32[]{:T(128)}, f32[6,1,1176,64]{2,3,1,0:T(8,128)}, ...), condition=%wide.region_14.15_spmd.clone.clone, body=%wide.region_12.14_spmd.clone.sunk.clone | while | flops 898933184 | bytes 44843632 | solution.py:73
  149.3 2.9 fusion.147
  155.2 2.7 fusion.149
  162.4 2.9 fusion.147
  168.4 2.7 fusion.149
  175.6 2.9 fusion.147
  181.5 2.7 fusion.149
  188.7 2.9 fusion.147
  194.7 2.7 fusion.149
  201.8 2.9 fusion.147
  207.8 2.7 fusion.149
  214.9 2.9 fusion.147
  220.9 2.7 fusion.149
  228.0 9.3 %fusion.64 = bf16[768,768]{0,1:T(8,128)(2,1)} fusion(bf16[2352,768]{1,0:T(8,128)(2,1)} %all-gather.8.cloned.1.call-done, f32[2352,768]{1,0:T(8,128)} %get-tuple-element.296), kind=kOutput, calls=%fused_computation.109 | convolution fusion | flops 2791378944 | bytes 12017664 | tf_op jit(solution)/shard_map/dot_general | solution.py:28
  240.3 5.5 fusion.56
  247.7 4.4 convolution_convert_fusion.4
  253.8 4.1 fusion.68
  260.2 7.0 %convolution_add_fusion.1 = f32[1176,768]{1,0:T(8,128)} fusion(bf16[1176,1152]{0,1:T(8,128)(2,1)} %bitcast.277, bf16[768,1152]{1,0:T(8,128)(2,1)S(1)} %copy-done, bf16[1176,768]{1,0:T(8,128)(2,1)} %reduce-scatter.16.cloned.1.call-done), kind=kOutput, calls=%fused_computation.66 | convolution fusion | flops 2082705408 | bytes 9897984 | tf_op jit(solution)/shard_map/dot_general | solution.py:22
  268.5 4.5 convolution_add_fusion
  273.0 3.5 convolution_bitcast_fusion.2
  276.5 2.7 copy.56
  279.4 6.9 %fusion.78 = f32[768,1152]{1,0:T(8,128)} fusion(bf16[1176,768]{1,0:T(8,128)(2,1)} %multiply_convert_fusion.2, bf16[1176,1152]{0,1:T(8,128)(2,1)} %bitcast.278), kind=kOutput, calls=%fused_computation.144 | convolution fusion | flops 2080899072 | bytes 8054784 | tf_op jit(solution)/shard_map/dot_general | solution.py:28
  286.5 3.7 convert_element_type.106
  291.4 40.1 %psum.15 = f32[2,64]{1,0:T(2,128)} all-reduce(f32[2,64]{1,0:T(2,128)S(1)} %pad_maximum_fusion.1), channel_id=1, replica_groups=mesh['dp'=8,'hg'=2,'hid'=2] {'dp','hg','hid'}, use_global_device_ids=true, to_apply=%region_28.29 | all-reduce | flops 128 | bytes 1024 | tf_op jit(solution)/shard_map/psum | solution.py:160
  333.4 37.4 %reduce-scatter.20.cloned.1.call-done = bf16[96,768]{1,0:T(8,128)(2,1)} async-done(((bf16[768,768]{1,0:T(8,128)(2,1)}), bf16[96,768]{1,0:T(8,128)(2,1)}) %reduce-scatter.20.cloned.1.call-update) | async-done | bytes 147472 | tf_op jit(solution)/shard_map/reduce_scatter | solution.py:153
  372.5 95.6 %all-reduce.3.cloned.1.call-done = f32[1176,768]{1,0:T(8,128)} async-done(((f32[1176,768]{1,0:T(8,128)}), f32[1176,768]{1,0:T(8,128)}) %all-reduce.3.cloned.1.call-update) | async-done | bytes 3612688 | tf_op jit(solution)/shard_map/psum | solution.py:142
  468.1 4.1 multiply_reduce_fusion.1
  472.2 33.2 %all-reduce = f32[768]{0:T(1024)S(1)} all-reduce(f32[768]{0:T(1024)S(1)} %get-tuple-element.240), channel_id=5, replica_groups=mesh['dp'=8,'hg'=2,'hid'=2] {'dp','hid'}, use_global_device_ids=true, to_apply=%region_24.25.clone | all-reduce | flops 768 | bytes 6144
  506.0 4.7 add_convert_fusion
  510.7 8.4 %reduce-scatter.14.cloned.1.call-done = f32[1176,384]{1,0:T(8,128)} async-done(((f32[1176,768]{1,0:T(8,128)}), f32[1176,384]{1,0:T(8,128)}) %reduce-scatter.14.cloned.1.call-update) | async-done | bytes 1806352 | tf_op jit(solution)/shard_map/reduce_scatter | solution.py:108
  519.1 3.1 add_convert_fusion.1
  522.2 58.9 %reduce-scatter.22.cloned.1.call-done = f32[48,384]{1,0:T(8,128)} async-done(((f32[768,384]{1,0:T(8,128)}), f32[48,384]{1,0:T(8,128)}) %reduce-scatter.22.cloned.1.call-update) | async-done | bytes 73744
  581.1 71.6 %reduce-scatter.18.cloned.1.call-done = f32[48,1152]{1,0:T(8,128)} async-done(((f32[768,1152]{1,0:T(8,128)}), f32[48,1152]{1,0:T(8,128)}) %reduce-scatter.18.cloned.1.call-update) | async-done | bytes 221200 | tf_op jit(solution)/shard_map/reduce_scatter | solution.py:148
  (187 shorter events, 105.2 us)
Async XLA Ops:
  7.2 40.9 %copy-start = (bf16[768,1152]{1,0:T(8,128)(2,1)S(1)}, bf16[768,1152]{1,0:T(8,128)(2,1)}, u32[]{:S(2)}) copy-start(bf16[768,1152]{1,0:T(8,128)(2,1)} %param.16) | copy-start | bytes 5308420
  7.2 35.0 %all-gather.6.cloned.1.call-start = ((), (), s32[]{:S(2)}) async-start(), calls=%async_computation.10 | async-start | bytes 2709504 | tf_op jit(solution)/shard_map/all_gather | solution.py:112
  7.9 63.1 %all-gather.8.cloned.1.call-start = ((), (), s32[]{:S(2)}) async-start(), calls=%async_computation.11 | async-start | bytes 5419008 | tf_op jit(solution)/shard_map/all_gather | solution.py:134
  42.2 37.2 %all-gather.4.cloned.1.call-start = ((), (), s32[]{:S(2)}) async-start(), calls=%async_computation.7 | async-start | bytes 5419008 | tf_op jit(solution)/shard_map/all_gather | solution.py:102
  42.2 2.6 copy-start.2
  43.0 2.5 copy-start.22
  44.9 0.7 copy-start.18
  45.6 0.6 copy-start.20
  48.0 212.2 %reduce-scatter.16.cloned.1.call-start = ((), (), s32[]{:S(2)}) async-start(), calls=%async_computation.12 | async-start | bytes 5419008 | tf_op jit(solution)/shard_map/reduce_scatter | solution.py:139
  52.1 2.7 copy-start.1
  52.2 2.9 copy-start.27
  55.0 6.6 %copy-start.9 = (f32[1176,6]{0,1:T(8,128)}, f32[1176,6]{0,1:T(8,128)S(1)}, u32[]{:S(2)}) copy-start(f32[1176,6]{0,1:T(8,128)S(1)} %broadcast_multiply_fusion.4) | copy-start | bytes 84676
  55.1 6.6 copy-start.24
  55.1 6.6 copy-start.11
  57.8 3.8 copy-start.13
  57.8 3.8 copy-start.15
  70.3 9.0 %copy-start.3 = (bf16[6,1,1176,64]{2,3,1,0:T(8,128)(2,1)}, bf16[6,1,1176,64]{2,3,1,0:T(8,128)(2,1)S(1)}, u32[]{:S(2)}) copy-start(bf16[6,1,1176,64]{2,3,1,0:T(8,128)(2,1)S(1)} %fusion.75) | copy-start | bytes 2709508
  79.3 13.2 %copy-start.29 = (bf16[768,768]{1,0:T(8,128)(2,1)S(1)}, bf16[768,768]{1,0:T(8,128)(2,1)}, u32[]{:S(2)}) copy-start(bf16[768,768]{1,0:T(8,128)(2,1)} %param.19) | copy-start | bytes 3538948
  90.6 1.9 copy-start.31
  97.1 1.2 copy-start.7
  97.1 170.2 %reduce-scatter.12.cloned.1.call-start = ((), (), s32[]{:S(2)}) async-start(), calls=%async_computation.8 | async-start | bytes 5419008 | tf_op jit(solution)/shard_map/reduce_scatter | solution.py:105
  98.3 34.2 %copy-start.17 = (bf16[768,384]{1,0:T(8,128)(2,1)S(1)}, bf16[768,384]{1,0:T(8,128)(2,1)}, u32[]{:S(2)}) copy-start(bf16[768,384]{1,0:T(8,128)(2,1)} %param.18) | copy-start | bytes 1769476
  131.9 4.1 copy-start.5
  147.9 1.2 copy-start.4
  147.9 183.6 %reduce-scatter.24.cloned.1.call-start = ((), (), s32[]{:S(2)}) async-start(), calls=%async_computation.17 | async-start | bytes 1327104
  237.3 2.9 copy-start.10
  237.3 2.9 copy-start.12
  237.3 2.9 copy-start.14
  237.3 3.0 copy-start.16
  237.3 3.0 copy-start.25
  239.8 131.1 %reduce-scatter.20.cloned.1.call-start = ((), (), s32[]{:S(2)}) async-start(), calls=%async_computation.15 | async-start | bytes 1327104 | tf_op jit(solution)/shard_map/reduce_scatter | solution.py:153
  240.3 7.4 %copy-start.28 = (bf16[2352,768]{1,0:T(8,128)(2,1)S(1)}, bf16[2352,768]{1,0:T(8,128)(2,1)}, u32[]{:S(2)}) copy-start(bf16[2352,768]{1,0:T(8,128)(2,1)} %all-gather.4.cloned.1.call-done) | copy-start | bytes 10838020
  240.3 7.4 %copy-start.32 = (bf16[2352,768]{1,0:T(8,128)(2,1)S(1)}, bf16[2352,768]{1,0:T(8,128)(2,1)}, u32[]{:S(2)}) copy-start(bf16[2352,768]{1,0:T(8,128)(2,1)} %copy-done.31) | copy-start | bytes 10838020
  252.2 216.0 %all-reduce.3.cloned.1.call-start = ((), (), s32[]{:S(2)}) async-start(), calls=%async_computation.13 | async-start | bytes 7225344 | tf_op jit(solution)/shard_map/psum | solution.py:142
  252.2 1.6 copy-start.8
  267.2 1.2 copy-start.6
  267.3 251.8 %reduce-scatter.14.cloned.1.call-start = ((), (), s32[]{:S(2)}) async-start(), calls=%async_computation.9 | async-start | bytes 5419008 | tf_op jit(solution)/shard_map/reduce_scatter | solution.py:108
  273.0 308.2 %reduce-scatter.22.cloned.1.call-start = ((), (), s32[]{:S(2)}) async-start(), calls=%async_computation.16 | async-start | bytes 1253376
  279.2 373.6 %reduce-scatter.18.cloned.1.call-start = ((), (), s32[]{:S(2)}) async-start(), calls=%async_computation.14 | async-start | bytes 3760128 | tf_op jit(solution)/shard_map/reduce_scatter | solution.py:148
  286.4 3.7 copy-start.30
  286.4 5.0 copy-start.26
  286.4 181.7 %copy-start.19 = (f32[1176]{0:T(1024)S(1)}, f32[1176]{0:T(1024)}, u32[]{:S(2)}) copy-start(f32[1176]{0:T(1024)} %copy-done.18) | copy-start | bytes 14116
  286.4 181.7 %copy-start.21 = (f32[1176]{0:T(1024)S(1)}, f32[1176]{0:T(1024)}, u32[]{:S(2)}) copy-start(f32[1176]{0:T(1024)} %copy-done.20) | copy-start | bytes 14116
  286.5 181.7 %copy-start.23 = (f32[768]{0:T(1024)S(1)}, f32[768]{0:T(1024)}, u32[]{:S(2)}) copy-start(f32[768]{0:T(1024)} %copy-done.22) | copy-start | bytes 9220
Sparse Core Ops, SparseCore 0:
  9.6 32.5 all-gather.5
  43.7 12.8 all-gather.7
  58.7 13.9 all-gather.3
  97.2 11.6 reduce-scatter.15
  148.0 11.8 reduce-scatter.11
  239.9 64.4 reduce-scatter.23
  307.8 63.0 reduce-scatter.19
  373.2 94.9 all-reduce.2
  470.4 48.6 reduce-scatter.13
  523.1 57.9 reduce-scatter.21
  585.6 67.1 reduce-scatter.17
where the time goes:
time: 666 us; the launch traced here: 659 us
  waiting for transfers between devices  307 us (46%)
  matrix products  178 us (27%)
  blocking collectives  73.3 us (11%)
  other arithmetic  52.7 us (8%)
  local copies, waits for them, and re-layouts  31.3 us (5%)
  between operations  15.9 us (2%)
    psum x1, waiting for transfers between devices, shards(): grad_normed = lax.psum(grad_normed_att + grad_normed_mlp, 'hg')  95.6 us
    reduce_scatter x1, waiting for transfers between devices, shards(): lax.psum_scatter(grad_w_qkv, ('dp', 'hid'), scatter_dimension=0, tiled=True)  71.6 us
    unnamed x13, waiting for transfers between devices  59.8 us
    psum x1, blocking collectives, shards(): qk_gains_grad = lax.psum(qk_partial, ('dp', 'hg', 'hid'))  40.1 us
    reduce_scatter x1, waiting for transfers between devices, shards(): lax.psum_scatter(grad_w_in.astype(jnp.bfloat16), 'dp', scatter_dimension=...  37.4 us
    all_gather x1, waiting for transfers between devices, shards(): grad_out = lax.all_gather(cotangent, 'hg', axis=1, tiled=True)  34.2 us
    unnamed x1, blocking collectives  33.2 us
    dot_general x12, matrix products, masked_scores(): jnp.einsum('gqe,gke->gqk', queries, keys_in, preferred_element_type=jnp.f...  32.3 us
  transfers between devices with their start and end apart: 11, of which 6 were waited for; matrix products, arithmetic and copies ran while one was open for 36% of the time, Pallas kernels for 0%

commit v1 on v0

--- a/solution.py
+++ b/solution.py
@@ -109,7 +109,14 @@
     out_cols = width // lax.axis_size("hg")
     input_cols = lax.dynamic_slice_in_dim(inputs, lax.axis_index("hg") * out_cols, out_cols, 1)
     output = (input_cols + mixed).astype(jnp.bfloat16)
-    grad_out = lax.all_gather(cotangent, "hg", axis=1, tiled=True)
+    ways, here = (lax.axis_size("hg"), lax.axis_index("hg"))
+    grad_out, reach = (cotangent, 1)
+    while reach < ways:
+        theirs = lax.ppermute(grad_out, "hg", [(d, d ^ reach) for d in range(ways)])
+        mine_first = jnp.concatenate([grad_out, theirs], axis=1)
+        theirs_first = jnp.concatenate([theirs, grad_out], axis=1)
+        grad_out = jnp.where(here & reach == 0, mine_first, theirs_first)
+        reach = 2 * reach
     grad_w_out = rows_t(grad_out, attended_low)
     grad_attended = jnp.dot(grad_out, w_out_t, preferred_element_type=jnp.float32)
     grad_att_low = (

time: 666 us -> 647 us (0.971)
  waiting for transfers between devices: 307 us -> 284 us
  other arithmetic: 52.7 us -> 62.7 us
  local copies, waits for them, and re-layouts: 31.3 us -> 21.3 us
    reduce_scatter x0 -> x2, waiting for transfers between devices: none -> 98.4 us  [the longest x1 59.2 us: shards(): lax.psum_scatter(grad_w_out, ('dp', 'hid'), scatter_dimension=0, tiled=True)]
    unnamed x13 -> x10, waiting for transfers between devices: 59.8 us -> 0.16 us
    reduce_scatter x1, waiting for transfers between devices: 37.4 us -> 0.01 us  [shards(): lax.psum_scatter(grad_w_in.astype(jnp.bfloat16), 'dp', scatter_dimension=...]
    all_gather x1 -> x0, waiting for transfers between devices: 34.2 us -> none  [shards(): grad_out = lax.all_gather(cotangent, 'hg', axis=1, tiled=True)]
    ppermute x0 -> x1, waiting for transfers between devices: none -> 9.77 us  [shards(): theirs = lax.ppermute(grad_out, 'hg', [(d, d ^ reach) for d in range(ways)])]
    unnamed x75 -> x73, local copies, waits for them, and re-layouts: 24.8 us -> 15.1 us
  transfers between devices with their start and end apart: 11 -> 11, of which waited for: 6 -> 6; matrix products, arithmetic and copies ran while one was open for 36% -> 37% of each run, Pallas kernels for 0% -> 0%
where the time goes in v1:
time: 647 us; the launch traced here: 641 us
  waiting for transfers between devices  284 us (44%)
  matrix products  178 us (28%)
  blocking collectives  74 us (11%)
  other arithmetic  62.7 us (10%)
  local copies, waits for them, and re-layouts  21.3 us (3%)
  between operations  16.1 us (2%)
    psum x1, waiting for transfers between devices, shards(): grad_normed = lax.psum(grad_normed_att + grad_normed_mlp, 'hg')  95.7 us
    reduce_scatter x1, waiting for transfers between devices, shards(): lax.psum_scatter(grad_w_qkv, ('dp', 'hid'), scatter_dimension=0, tiled=True)  71.3 us
    reduce_scatter x1, waiting for transfers between devices, shards(): lax.psum_scatter(grad_w_out, ('dp', 'hid'), scatter_dimension=0, tiled=True)  59.2 us
    psum x1, blocking collectives, shards(): qk_gains_grad = lax.psum(qk_partial, ('dp', 'hg', 'hid'))  40.8 us
    reduce_scatter x1, waiting for transfers between devices, shards(): lax.psum_scatter(grad_w_back.astype(jnp.bfloat16), 'dp', scatter_dimensio...  39.2 us
    unnamed x1, blocking collectives  33.2 us
    dot_general x12, matrix products, masked_scores(): jnp.einsum('gqe,gke->gqk', queries, keys_in, preferred_element_type=jnp.f...  32.4 us
    dot_general x4, matrix products, times_t(): lax.dot_general(left, right, (((1,), (1,)), ((), ())), preferred_element_...  25.6 us
  transfers between devices with their start and end apart: 11, of which 6 were waited for; matrix products, arithmetic and copies ran while one was open for 37% of the time, Pallas kernels for 0%

profile of v1, /device:TPU:0, one launch (start us, length us, event | category | flops | bytes accessed | tf_op | source)
XLA Modules:
  0.0 641.1 jit_solution(11084577099518265443)
XLA Ops:
  13.2 3.0 collective-permute-start
  16.2 6.5 %fusion.75 = f32[1176,1152]{0,1:T(8,128)} fusion(bf16[1176,768]{1,0:T(8,128)(2,1)} %multiply_convert_fusion.2, bf16[768,1152]{1,0:T(8,128)(2,1)S(1)} %copy-done), kind=kOutput, calls=%fused_computation.141 | convolution fusion | flops 2080899072 | bytes 8994816 | tf_op jit(solution)/shard_map/dot_general | solution.py:89
  26.6 9.8 %collective-permute-done = bf16[1176,384]{1,0:T(8,128)(2,1)} collective-permute-done((bf16[1176,384]{1,0:T(8,128)(2,1)S(1)}, bf16[1176,384]{1,0:T(8,128)(2,1)}, u32[]{:S(2)}, u32[]{:S(2)}) %collective-permute-start) | collective-permute-done | bytes 903200 | tf_op jit(solution)/shard_map/ppermute | solution.py:115
  36.4 3.1 maximum_select_fusion
  40.1 2.7 multiply_reduce_fusion.6
  42.8 3.8 fusion.65
  46.6 2.8 copy.39
  55.2 8.3 %fusion.76 = f32[2352,768]{1,0:T(8,128)} fusion(bf16[2352,768]{1,0:T(8,128)(2,1)} %all-gather.3.cloned.1.call-done, bf16[768,768]{1,0:T(8,128)(2,1)} %param.19), kind=kOutput, calls=%fused_computation.142 | convolution fusion | flops 2774532096 | bytes 12017664 | tf_op jit(solution)/shard_map/dot_general | solution.py:103
  63.5 9.4 %fusion.54 = bf16[2352,768]{1,0:T(8,128)(2,1)S(1)} fusion(f32[2352,768]{1,0:T(8,128)} %fusion.76, bf16[2352,768]{1,0:T(8,128)(2,1)} %all-gather.5.cloned.1.call-done, bf16[768,768]{1,0:T(8,128)(2,1)} %param.20), kind=kOutput, calls=%fused_computation.61 | convolution fusion | flops 2810658816 | bytes 15630336 | tf_op jit(solution)/shard_map/dot_general | solution.py:142
  74.8 4.5 convolution_convert_fusion
  80.5 33.6 %while.30 = (s32[]{:T(128)}, bf16[6,1,1176,64]{2,3,1,0:T(8,128)(2,1)S(1)}, f32[6,1,1176]{2,1,0:T(1,128)S(1)}, bf16[6,1,1176,64]{3,2,1,0:T(8,128)(2,1)}, bf16[6,1...) while((s32[]{:T(128)}, ...), condition=%wide.region_9.10_spmd.clone.clone, body=%wide.region_6.9_spmd.clone.sunk.clone | while | flops 366487456 | bytes 18392728 | solution.py:73
  80.5 2.6 fusion.136
  86.2 2.7 fusion.136
  91.9 2.5 fusion.136
  114.7 3.5 convolution_convert_fusion.2
  120.5 9.6 %convolution_convert_fusion.1 = bf16[2352,768]{1,0:T(8,128)(2,1)} fusion(bf16[768,768]{1,0:T(8,128)(2,1)} %param.20, f32[2352,768]{1,0:T(8,128)} %fusion.76), kind=kOutput, calls=%fused_computation.64 | convolution fusion | flops 2792595456 | bytes 12017664 | tf_op jit(solution)/shard_map/dot_general | solution.py:22
  131.4 78.8 %while.31 = (s32[]{:T(128)}, f32[6,1,1176,64]{2,3,1,0:T(8,128)}, f32[6,1,1176,64]{2,3,1,0:T(8,128)}, bf16[6,1,1176,64]{2,3,1,0:T(8,128)(2,1)S(1)}, bf16[6,1,1176...) while((s32[]{:T(128)}, f32[6,1,1176,64]{2,3,1,0:T(8,128)}, ...), condition=%wide.region_14.15_spmd.clone.clone, body=%wide.region_12.14_spmd.clone.sunk.clone | while | flops 898933184 | bytes 44843632 | solution.py:73
  131.4 2.9 fusion.147
  137.3 2.8 fusion.149
  144.6 2.9 fusion.147
  150.6 2.7 fusion.149
  157.7 2.9 fusion.147
  163.7 2.7 fusion.149
  170.9 2.9 fusion.147
  176.8 2.7 fusion.149
  184.0 2.9 fusion.147
  189.9 2.7 fusion.149
  197.1 2.9 fusion.147
  203.0 2.7 fusion.149
  210.2 5.6 fusion.56
  215.9 4.4 convolution_convert_fusion.4
  224.9 8.7 %convolution_convert_fusion.3 = bf16[768,768]{1,0:T(8,128)(2,1)} fusion(bf16[2352,768]{1,0:T(8,128)(2,1)} %all-gather.5.cloned.1.call-done, f32[2352,768]{1,0:T(8,128)} %fusion.76), kind=kOutput, calls=%fused_computation.108 | convolution fusion | flops 2791378944 | bytes 12017664 | tf_op jit(solution)/shard_map/dot_general | solution.py:28
  235.2 4.1 fusion.67
  241.7 7.0 %convolution_add_fusion.1 = f32[1176,768]{1,0:T(8,128)} fusion(bf16[1176,1152]{0,1:T(8,128)(2,1)} %bitcast.271, bf16[768,1152]{1,0:T(8,128)(2,1)S(1)} %copy-done, bf16[1176,768]{1,0:T(8,128)(2,1)} %reduce-scatter.12.cloned.1.call-done), kind=kOutput, calls=%fused_computation.66 | convolution fusion | flops 2082705408 | bytes 9897984 | tf_op jit(solution)/shard_map/dot_general | solution.py:22
  249.9 4.5 convolution_add_fusion
  254.5 3.7 fusion.78
  258.5 7.0 %fusion.77 = f32[768,1152]{1,0:T(8,128)} fusion(bf16[1176,768]{1,0:T(8,128)(2,1)} %multiply_convert_fusion.2, bf16[1176,1152]{0,1:T(8,128)(2,1)} %bitcast.272), kind=kOutput, calls=%fused_computation.143 | convolution fusion | flops 2080899072 | bytes 8054784 | tf_op jit(solution)/shard_map/dot_general | solution.py:28
  265.5 3.7 convert_element_type.103
  270.5 40.8 %psum.15 = f32[2,64]{1,0:T(2,128)} all-reduce(f32[2,64]{1,0:T(2,128)S(1)} %pad_maximum_fusion.1), channel_id=1, replica_groups=mesh['dp'=8,'hg'=2,'hid'=2] {'dp','hg','hid'}, use_global_device_ids=true, to_apply=%region_28.29 | all-reduce | flops 128 | bytes 1024 | tf_op jit(solution)/shard_map/psum | solution.py:167
  313.0 39.2 %reduce-scatter.20.cloned.1.call-done = bf16[96,768]{1,0:T(8,128)(2,1)} async-done(((bf16[768,768]{1,0:T(8,128)(2,1)}), bf16[96,768]{1,0:T(8,128)(2,1)}) %reduce-scatter.20.cloned.1.call-update) | async-done | bytes 147472 | tf_op jit(solution)/shard_map/reduce_scatter | solution.py:163
  353.8 95.7 %all-reduce.3.cloned.1.call-done = f32[1176,768]{1,0:T(8,128)} async-done(((f32[1176,768]{1,0:T(8,128)}), f32[1176,768]{1,0:T(8,128)}) %all-reduce.3.cloned.1.call-update) | async-done | bytes 3612688 | tf_op jit(solution)/shard_map/psum | solution.py:149
  449.5 4.1 multiply_reduce_fusion.1
  453.6 33.2 %all-reduce = f32[768]{0:T(1024)S(1)} all-reduce(f32[768]{0:T(1024)S(1)} %get-tuple-element.216), channel_id=5, replica_groups=mesh['dp'=8,'hg'=2,'hid'=2] {'dp','hid'}, use_global_device_ids=true, to_apply=%region_24.25.clone | all-reduce | flops 768 | bytes 6144
  487.4 4.7 add_convert_fusion
  492.1 8.4 %reduce-scatter.10.cloned.1.call-done = f32[1176,384]{1,0:T(8,128)} async-done(((f32[1176,768]{1,0:T(8,128)}), f32[1176,384]{1,0:T(8,128)}) %reduce-scatter.10.cloned.1.call-update) | async-done | bytes 1806352 | tf_op jit(solution)/shard_map/reduce_scatter | solution.py:108
  500.5 3.1 add_convert_fusion.1
  503.6 59.2 %reduce-scatter.16.cloned.1.call-done = f32[48,384]{1,0:T(8,128)} async-done(((f32[768,384]{1,0:T(8,128)}), f32[48,384]{1,0:T(8,128)}) %reduce-scatter.16.cloned.1.call-update) | async-done | bytes 73744 | tf_op jit(solution)/shard_map/reduce_scatter | solution.py:156
  562.8 71.3 %reduce-scatter.14.cloned.1.call-done = f32[48,1152]{1,0:T(8,128)} async-done(((f32[768,1152]{1,0:T(8,128)}), f32[48,1152]{1,0:T(8,128)}) %reduce-scatter.14.cloned.1.call-update) | async-done | bytes 221200 | tf_op jit(solution)/shard_map/reduce_scatter | solution.py:155
  (186 shorter events, 107.9 us)
Async XLA Ops:
  7.2 9.0 %copy-start = (bf16[768,1152]{1,0:T(8,128)(2,1)S(1)}, bf16[768,1152]{1,0:T(8,128)(2,1)}, u32[]{:S(2)}) copy-start(bf16[768,1152]{1,0:T(8,128)(2,1)} %param.16) | copy-start | bytes 5308420
  7.2 2.9 copy-start.27
  7.2 48.0 %all-gather.3.cloned.1.call-start = ((), (), s32[]{:S(2)}) async-start(), calls=%async_computation.7 | async-start | bytes 5419008 | tf_op jit(solution)/shard_map/all_gather | solution.py:102
  7.2 2.2 copy-start.1
  9.4 0.8 copy-start.18
  10.1 3.1 copy-start.12
  10.1 0.6 copy-start.20
  10.7 0.6 copy-start.22
  13.1 50.4 %all-gather.5.cloned.1.call-start = ((), (), s32[]{:S(2)}) async-start(), calls=%async_computation.10 | async-start | bytes 5419008 | tf_op jit(solution)/shard_map/all_gather | solution.py:141
  13.2 23.2 %collective-permute-start = (bf16[1176,384]{1,0:T(8,128)(2,1)S(1)}, bf16[1176,384]{1,0:T(8,128)(2,1)}, u32[]{:S(2)}, u32[]{:S(2)}) collective-permute-start(bf16[1176,384]{1,0:T(8,128)(2,1)S(1)} %copy-done.12), channel_id=1, source_target_pairs={{0,2},{2,0},{1,3},{3,1},{4,6},{6,4},{5,7},{7,5},{8,10},{10,8},{9,1... | collective-permute-start | bytes 2709512 | tf_op jit(solution)/shard_map/ppermute | solution.py:115
  26.6 13.5 %copy-start.28 = (bf16[2,64]{1,0:T(2,128)(2,1)S(1)}, bf16[2,64]{1,0:T(2,128)(2,1)}, u32[]{:S(2)}) copy-start(bf16[2,64]{1,0:T(2,128)(2,1)} %param.17) | copy-start | bytes 772
  26.6 16.2 %copy-start.8 = (f32[1176,6]{0,1:T(8,128)}, f32[1176,6]{0,1:T(8,128)S(1)}, u32[]{:S(2)}) copy-start(f32[1176,6]{0,1:T(8,128)S(1)} %broadcast_multiply_fusion.4) | copy-start | bytes 84676
  39.4 202.3 %reduce-scatter.12.cloned.1.call-start = ((), (), s32[]{:S(2)}) async-start(), calls=%async_computation.11 | async-start | bytes 5419008 | tf_op jit(solution)/shard_map/reduce_scatter | solution.py:146
  40.0 6.6 %copy-start.24 = (f32[64]{0:T(128)}, f32[64]{0:T(128)S(1)}, u32[]{:S(2)}) copy-start(f32[64]{0:T(128)S(1)} %get-tuple-element.269) | copy-start | bytes 772
  40.1 6.6 %copy-start.10 = (f32[1176,6]{0,1:T(8,128)}, f32[1176,6]{0,1:T(8,128)S(1)}, u32[]{:S(2)}) copy-start(f32[1176,6]{0,1:T(8,128)S(1)} %broadcast_multiply_fusion.5) | copy-start | bytes 84676
  42.8 3.8 copy-start.13
  42.8 3.8 copy-start.15
  54.5 9.0 %copy-start.2 = (bf16[6,1,1176,64]{2,3,1,0:T(8,128)(2,1)}, bf16[6,1,1176,64]{2,3,1,0:T(8,128)(2,1)S(1)}, u32[]{:S(2)}) copy-start(bf16[6,1,1176,64]{2,3,1,0:T(8,128)(2,1)S(1)} %fusion.74) | copy-start | bytes 2709508
  63.5 11.3 %copy-start.30 = (bf16[768,768]{1,0:T(8,128)(2,1)S(1)}, bf16[768,768]{1,0:T(8,128)(2,1)}, u32[]{:S(2)}) copy-start(bf16[768,768]{1,0:T(8,128)(2,1)} %param.19) | copy-start | bytes 3538948
  72.9 1.9 copy-start.32
  79.3 1.2 copy-start.6
  79.4 169.5 %reduce-scatter.8.cloned.1.call-start = ((), (), s32[]{:S(2)}) async-start(), calls=%async_computation.8 | async-start | bytes 5419008 | tf_op jit(solution)/shard_map/reduce_scatter | solution.py:105
  80.5 34.2 %copy-start.17 = (bf16[768,384]{1,0:T(8,128)(2,1)S(1)}, bf16[768,384]{1,0:T(8,128)(2,1)}, u32[]{:S(2)}) copy-start(bf16[768,384]{1,0:T(8,128)(2,1)} %param.18) | copy-start | bytes 1769476
  114.1 4.1 copy-start.4
  130.1 1.2 copy-start.3
  130.2 181.2 %reduce-scatter.18.cloned.1.call-start = ((), (), s32[]{:S(2)}) async-start(), calls=%async_computation.15 | async-start | bytes 1327104 | tf_op jit(solution)/shard_map/reduce_scatter | solution.py:160
  131.3 78.8 %copy-start.9 = (f32[1176,6]{0,1:T(8,128)S(1)}, f32[1176,6]{0,1:T(8,128)}, u32[]{:S(2)}) copy-start(f32[1176,6]{0,1:T(8,128)} %copy-done.8) | copy-start | bytes 84676
  131.3 78.8 %copy-start.11 = (f32[1176,6]{0,1:T(8,128)S(1)}, f32[1176,6]{0,1:T(8,128)}, u32[]{:S(2)}) copy-start(f32[1176,6]{0,1:T(8,128)} %copy-done.10) | copy-start | bytes 84676
  131.3 78.8 %copy-start.14 = (f32[1176,6]{0,1:T(8,128)S(1)}, f32[1176,6]{0,1:T(8,128)}, u32[]{:S(2)}) copy-start(f32[1176,6]{0,1:T(8,128)} %copy-done.13) | copy-start | bytes 84676
  131.3 78.8 %copy-start.16 = (f32[1176,6]{0,1:T(8,128)S(1)}, f32[1176,6]{0,1:T(8,128)}, u32[]{:S(2)}) copy-start(f32[1176,6]{0,1:T(8,128)} %copy-done.15) | copy-start | bytes 84676
  131.3 78.8 %copy-start.25 = (f32[64]{0:T(128)S(1)}, f32[64]{0:T(128)}, u32[]{:S(2)}) copy-start(f32[64]{0:T(128)} %copy-done.24) | copy-start | bytes 772
  210.2 5.7 copy-start.29
  210.2 5.7 copy-start.33
  220.3 131.9 %reduce-scatter.20.cloned.1.call-start = ((), (), s32[]{:S(2)}) async-start(), calls=%async_computation.16 | async-start | bytes 1327104 | tf_op jit(solution)/shard_map/reduce_scatter | solution.py:163
  233.6 215.9 %all-reduce.3.cloned.1.call-start = ((), (), s32[]{:S(2)}) async-start(), calls=%async_computation.12 | async-start | bytes 7225344 | tf_op jit(solution)/shard_map/psum | solution.py:149
  233.7 1.6 copy-start.7
  248.7 1.2 copy-start.5
  248.8 251.7 %reduce-scatter.10.cloned.1.call-start = ((), (), s32[]{:S(2)}) async-start(), calls=%async_computation.9 | async-start | bytes 5419008 | tf_op jit(solution)/shard_map/reduce_scatter | solution.py:108
  254.5 308.3 %reduce-scatter.16.cloned.1.call-start = ((), (), s32[]{:S(2)}) async-start(), calls=%async_computation.14 | async-start | bytes 1253376 | tf_op jit(solution)/shard_map/reduce_scatter | solution.py:156
  258.3 375.8 %reduce-scatter.14.cloned.1.call-start = ((), (), s32[]{:S(2)}) async-start(), calls=%async_computation.13 | async-start | bytes 3760128 | tf_op jit(solution)/shard_map/reduce_scatter | solution.py:155
  265.5 3.8 copy-start.31
  265.5 5.0 copy-start.26
  265.5 184.0 %copy-start.19 = (f32[1176]{0:T(1024)S(1)}, f32[1176]{0:T(1024)}, u32[]{:S(2)}) copy-start(f32[1176]{0:T(1024)} %copy-done.18) | copy-start | bytes 14116
  265.5 184.0 %copy-start.21 = (f32[1176]{0:T(1024)S(1)}, f32[1176]{0:T(1024)}, u32[]{:S(2)}) copy-start(f32[1176]{0:T(1024)} %copy-done.20) | copy-start | bytes 14116
  265.5 184.0 %copy-start.23 = (f32[768]{0:T(1024)S(1)}, f32[768]{0:T(1024)}, u32[]{:S(2)}) copy-start(f32[768]{0:T(1024)} %copy-done.22) | copy-start | bytes 9220
Sparse Core Ops, SparseCore 0:
  13.3 15.4 all-gather.2
  39.6 14.2 all-gather.4
  79.5 12.9 reduce-scatter.11
  130.3 12.9 reduce-scatter.7
  220.4 65.6 reduce-scatter.17
  289.3 62.8 reduce-scatter.19
  354.5 94.9 all-reduce.2
  451.8 48.6 reduce-scatter.9
  504.7 58.0 reduce-scatter.15
  567.1 66.9 reduce-scatter.13
